TPU v7x, 32 devices: a whole 2x2x4 slice. The times are simulated.
32 devices in a mesh: row: 8 (over z, y), col: 4 (over x, core).
Axes of the slice: x: 2, y: 2, z: 4, core: 2. Of those that a mesh axis runs over, the one named last changes fastest.
Arguments:
- ancestor_inverse: float32 [12288, 12288], P('row', 'col'), may hold values from -5 to 320, as said below
- panel_one: float32 [12288, 256], P(('row', 'col')), may hold values from -0.015625 to 0.015625
- struct_one: int32 [10752], replicated, may hold values from 0 to 12287, as said below
- lower_one: float32 [256, 256], replicated, may hold values from -1 to 2, as said below
- panel_two: float32 [12288, 256], P(('row', 'col')), may hold values from -0.015625 to 0.015625
- struct_two: int32 [9216], replicated, may hold values from 0 to 12287, as said below
- panel_above: float32 [256, 256], replicated, may hold values from -0.375 to 0.375
- lower_two: float32 [256, 256], replicated, may hold values from -1 to 2, as said below
- tile_owner: int32 [192, 1], P(('col', 'row')), may hold values from 0 to 3; in each aligned block of 6 rows (0 to 5, 6 to 11, ...) at most 2 rows name the same one
Outputs:
- inverse_one: float32 [12288, 256], P(('col', 'row'))
- diag_one: float32 [256, 256], replicated
- cross_two: float32 [256, 256], replicated
- diag_two: float32 [256, 256], replicated
- delivered: float32 [256, 64, 256], P(('row', 'col'))
Inputs may be any that keep to these rules, and one draw needn't show every extreme that they name: ancestor_inverse is exactly symmetric and positive definite. `struct_one`: 10752 distinct row numbers of the ancestor block. `struct_two`: 9216 distinct entries of struct_one. `lower_one`: lower triangular with a positive diagonal. `lower_two`: lower triangular with a positive diagonal. `tile_owner`: within each aligned block of 6 entries (the tiles of one device) no value appears more than 2 times; in some block a value appears exactly 2 times.
All inputs are finite; a program needn't handle non-finite values.
Results may differ from a plain program's by a relative error of at most 0.00007.
Values sent between devices are 32-bit elements; how exact they have to be, the bound alone decides.
A program may use at most 64 MiB of HBM per device.

v0:
```python
import jax
import jax.numpy as jnp
from jax import lax
from jax.sharding import PartitionSpec as P

ANC = 12288
CAP = 2


def matmul(left, right):
    return jnp.dot(left, right, precision=lax.Precision.HIGHEST, preferred_element_type=jnp.float32)


def contract_rows(left, right):
    return lax.dot_general(
        left,
        right,
        (((0,), (0,)), ((), ())),
        precision=lax.Precision.HIGHEST,
        preferred_element_type=jnp.float32,
    )


def product_term(ancestor_inverse, block_panel, placed_rows):
    return jnp.concatenate([contract_rows(ancestor_inverse, block_panel), placed_rows], axis=1)


def deliver(values, tile_owner, col_count):
    tile_count = tile_owner.shape[0]
    tile_rows = values.shape[0] // tile_count
    all_tiles = values.reshape(tile_count, tile_rows, values.shape[1])
    owner_col = tile_owner[:, 0]
    col_ids = jnp.arange(col_count, dtype=jnp.int32)
    onehot = (owner_col[:, None] == col_ids[None, :]).astype(jnp.int32)
    tile_rank = jnp.sum((jnp.cumsum(onehot, axis=0) - onehot) * onehot, axis=1)
    slot_index = jnp.arange(CAP, dtype=jnp.int32)
    select = (
        (owner_col[None, None, :] == col_ids[:, None, None])
        & (tile_rank[None, None, :] == slot_index[None, :, None])
    ).astype(jnp.float32)
    outgoing = jnp.einsum("cks,srb->ckrb", select, all_tiles, precision=lax.Precision.HIGHEST)
    incoming = lax.all_to_all(outgoing, "col", split_axis=0, concat_axis=0, tiled=True)
    return incoming.reshape(col_count * CAP, tile_rows, values.shape[1])


def local(
    ancestor_inverse,
    panel_one,
    struct_one,
    lower_one,
    panel_two,
    struct_two,
    panel_above,
    lower_two,
    tile_owner,
):
    row_count = lax.axis_size("row")
    col_count = lax.axis_size("col")
    row_index = lax.axis_index("row")
    col_index = lax.axis_index("col")
    block_ratio = row_count // col_count
    local_rows = panel_one.shape[0]
    inner_rows = ancestor_inverse.shape[0]
    column_rows = ancestor_inverse.shape[1]
    width = panel_one.shape[1]
    mask_one = jnp.zeros((ANC,), jnp.float32).at[struct_one].set(1.0)
    mask_two = jnp.zeros((ANC,), jnp.float32).at[struct_two].set(1.0)
    panel_start = (row_index * col_count + col_index) * local_rows
    result_start = (col_index * row_count + row_index) * local_rows
    local_one = panel_one * lax.dynamic_slice_in_dim(mask_one, panel_start, local_rows)[:, None]
    local_two = panel_two * lax.dynamic_slice_in_dim(mask_two, panel_start, local_rows)[:, None]
    result_mask_one = lax.dynamic_slice_in_dim(mask_one, result_start, local_rows)[:, None]
    result_mask_two = lax.dynamic_slice_in_dim(mask_two, result_start, local_rows)[:, None]
    owns_block = (row_index // block_ratio == col_index).astype(jnp.float32)
    block_offset = row_index % block_ratio * inner_rows

    def place(gathered):
        empty_rows = jnp.zeros((column_rows, gathered.shape[1]), jnp.float32)
        return lax.dynamic_update_slice_in_dim(empty_rows, gathered * owns_block, block_offset, 0)

    gathered_one = lax.all_gather(local_one, "col", axis=0, tiled=True)
    summed_one = lax.psum_scatter(
        product_term(ancestor_inverse, gathered_one, place(gathered_one)),
        "row",
        scatter_dimension=0,
        tiled=True,
    )
    gathered_two = lax.all_gather(local_two, "col", axis=0, tiled=True)
    summed_two = lax.psum_scatter(
        product_term(ancestor_inverse, gathered_two, place(gathered_two)),
        "row",
        scatter_dimension=0,
        tiled=True,
    )
    product_one = summed_one[:, :width]
    resident_one = summed_one[:, width:]
    product_two = summed_two[:, :width]
    resident_two = summed_two[:, width:]
    inverse_one = -product_one * result_mask_one
    partial_gram = contract_rows(resident_one, inverse_one)
    partial_cross = contract_rows(inverse_one, resident_two)
    gram_one, cross_sum = lax.psum((partial_gram, partial_cross), ("row", "col"))
    diag_one = matmul(lower_one.T, lower_one) - gram_one
    cross_two = -(cross_sum + matmul(diag_one, panel_above))
    inverse_two = -(product_two + matmul(inverse_one, panel_above)) * result_mask_two
    partial_second = contract_rows(resident_two, inverse_two)
    gram_two = lax.psum(partial_second, ("row", "col"))
    diag_two = matmul(lower_two.T, lower_two) - gram_two - matmul(panel_above.T, cross_two)
    delivered = deliver(inverse_two, tile_owner, col_count)
    return (inverse_one, diag_one, cross_two, diag_two, delivered)


def solution(mesh):
    return jax.shard_map(
        local,
        mesh=mesh,
        in_specs=(
            P("row", "col"),
            P(("row", "col"), None),
            P(),
            P(),
            P(("row", "col"), None),
            P(),
            P(),
            P(),
            P(("col", "row"), None),
        ),
        out_specs=(P(("col", "row"), None), P(), P(), P(), P(("row", "col"), None, None)),
        check_vma=False,
    )
```

profile of v0, /device:TPU:0, one launch (start us, length us, event | category | flops | bytes accessed | tf_op | source)
XLA Modules:
  0.0 510.6 jit_solution(6775725624319687121)
XLA Ops:
  7.2 0.8 compare_select_fusion
  8.1 1.2 copy.36
  9.2 39.8 %scatter_custom_fusion = f32[12288]{0:T(1024)S(1)} fusion(s32[10752]{0:T(1024)S(1)} %compare_select_fusion, f32[10752]{0:T(1024)S(1)} %broadcast.48, f32[]{:T(128)} %constant.23.clone.1), kind=kCustom, calls=%fused_computation.34 | custom fusion | bytes 49156 | tf_op jit(solution)/shard_map/scatter | solution.py:66
  49.2 0.8 broadcast_multiply_fusion.1
  50.0 1.2 copy.37
  51.2 0.8 compare_select_fusion.1
  52.0 34.2 %scatter_custom_fusion.1 = f32[12288]{0:T(1024)S(1)} fusion(s32[9216]{0:T(1024)S(1)} %compare_select_fusion.1, f32[9216]{0:T(1024)S(1)} %broadcast.49, f32[]{:T(128)} %constant.23.clone.1), kind=kCustom, calls=%fused_computation.32 | custom fusion | bytes 49156 | tf_op jit(solution)/shard_map/scatter | solution.py:67
  86.3 0.8 broadcast_multiply_fusion
  87.5 1.0 copy-done.1
  88.7 19.2 %convolution_bitcast_fusion.1 = f32[3072,256]{0,1:T(8,128)S(1)} fusion(f32[1536,256]{0,1:T(8,128)S(1)} %copy-done.1, f32[1536,3072]{1,0:T(8,128)} %param.9), kind=kOutput, calls=%fused_computation.5 | convolution fusion | flops 14495514624 | bytes 23592960 | tf_op jit(solution)/shard_map/dot_general | solution.py:15
  107.9 3.1 pad_maximum_fusion
  111.6 1.0 copy-done.2
  112.8 19.2 %convolution_bitcast_fusion = f32[3072,256]{0,1:T(8,128)S(1)} fusion(f32[1536,256]{0,1:T(8,128)S(1)} %copy-done.2, f32[1536,3072]{1,0:T(8,128)} %param.9), kind=kOutput, calls=%fused_computation.4 | convolution fusion | flops 14495514624 | bytes 23592960 | tf_op jit(solution)/shard_map/dot_general | solution.py:15
  132.0 3.0 pad_maximum_fusion.1
  136.0 96.0 %reduce-scatter.3.cloned.1.call-done = f32[384,512]{0,1:T(8,128)} async-done(((f32[3072,512]{0,1:T(8,128)}), f32[384,512]{0,1:T(8,128)}) %reduce-scatter.3.cloned.1.call-update) | async-done | bytes 786448 | tf_op jit(solution)/shard_map/reduce_scatter | solution.py:82
  232.0 1.0 fusion.9
  233.0 119.7 %reduce-scatter.5.cloned.1.call-done = f32[384,512]{0,1:T(8,128)} async-done(((f32[3072,512]{0,1:T(8,128)}), f32[384,512]{0,1:T(8,128)}) %reduce-scatter.5.cloned.1.call-update) | async-done | bytes 786448 | tf_op jit(solution)/shard_map/reduce_scatter | solution.py:89
  352.7 1.7 fusion.1
  354.6 0.7 fusion.4
  355.2 0.9 copy.42
  356.1 3.6 all-to-all-start
  359.8 1.3 fusion.10
  361.1 1.3 fusion.12
  362.5 1.3 fusion.7
  363.8 0.9 copy.43
  364.7 3.8 all-to-all-done
  368.5 128.8 %all-reduce.3.cloned.1.call-done = (f32[256,256]{1,0:T(8,128)}, f32[256,256]{1,0:T(8,128)}, f32[256,256]{1,0:T(8,128)}) async-done(((f32[256,256]{1,0:T(8,128)}, f32[256,256]{1,0:T(8,128)}, f32[256,256]{1,0:T(8,128)}), (f32[256,256]{1,0:T(8,128)}, f32[256,256]{1,0:T(8,128)}, f32[256,256]{1,0:T(8,128)})) %all-reduce.3.cloned.1.call-update) | async-done | bytes 786448 | tf_op jit(solution)/shard_map/psum | solution.py:102
  497.3 1.5 convolution_subtract_fusion.1
  498.8 1.4 fusion.3
  500.3 1.6 convolution_subtract_fusion
  502.0 1.3 fusion.2
  503.3 0.8 copy.59
  (44 shorter events, 2.7 us)
Async XLA Ops:
  7.2 345.5 %copy-start = (f32[256,256]{1,0:T(8,128)S(1)}, f32[256,256]{1,0:T(8,128)}, u32[]{:S(2)}) copy-start(f32[256,256]{1,0:T(8,128)} %param.15) | copy-start | bytes 786436
  7.2 80.0 %all-gather.3.cloned.1.call-start = ((), (), s32[]{:S(2)}) async-start(), calls=%async_computation.3 | async-start | bytes 1966080 | tf_op jit(solution)/shard_map/all_gather | solution.py:81
  50.0 61.3 %all-gather.5.cloned.1.call-start = ((), (), s32[]{:S(2)}) async-start(), calls=%async_computation.5 | async-start | bytes 1966080 | tf_op jit(solution)/shard_map/all_gather | solution.py:88
  87.1 144.9 %reduce-scatter.3.cloned.1.call-start = ((), (), s32[]{:S(2)}) async-start(), calls=%async_computation.4 | async-start | bytes 7077888 | tf_op jit(solution)/shard_map/reduce_scatter | solution.py:82
  87.2 1.4 copy-start.1
  111.0 241.7 %reduce-scatter.5.cloned.1.call-start = ((), (), s32[]{:S(2)}) async-start(), calls=%async_computation.6 | async-start | bytes 7077888 | tf_op jit(solution)/shard_map/reduce_scatter | solution.py:89
  111.3 1.4 copy-start.2
  135.1 0.7 copy-start.9
  352.7 7.1 %copy-start.3 = (f32[384,512]{0,1:T(8,128)S(1)}, f32[384,512]{0,1:T(8,128)}, u32[]{:S(2)}) copy-start(f32[384,512]{0,1:T(8,128)} %reduce-scatter.5.cloned.1.call-done) | copy-start | bytes 2359300
  354.4 8.1 %copy-start.8 = (f32[384,512]{0,1:T(8,128)S(1)}, f32[384,512]{0,1:T(8,128)}, u32[]{:S(2)}) copy-start(f32[384,512]{0,1:T(8,128)} %reduce-scatter.3.cloned.1.call-done) | copy-start | bytes 2359300
  356.1 141.1 %copy-start.4 = (f32[256,256]{1,0:T(8,128)S(1)}, f32[256,256]{1,0:T(8,128)}, u32[]{:S(2)}) copy-start(f32[256,256]{1,0:T(8,128)} %param.12) | copy-start | bytes 786436
  356.1 12.4 %all-to-all-start = ((f32[4,2,64,256]{3,2,1,0:T(8,128)}), f32[4,2,64,256]{3,2,1,0:T(8,128)S(1)}, u32[]{:S(2)}, u32[]{:S(2)}) async-start(f32[4,2,64,256]{3,2,1,0:T(8,128)} %copy.42), calls=%async_computation.2 | async-start | bytes 1048576 | tf_op jit(solution)/shard_map/all_to_all | solution.py:42
  359.8 137.5 %all-reduce.3.cloned.1.call-start = ((), (), s32[]{:S(2)}) async-start(), calls=%async_computation.7 | async-start | bytes 1572864 | tf_op jit(solution)/shard_map/psum | solution.py:102
  361.1 139.2 %copy-start.5 = (f32[256,256]{1,0:T(8,128)S(1)}, f32[256,256]{1,0:T(8,128)}, u32[]{:S(2)}) copy-start(f32[256,256]{1,0:T(8,128)} %param.16) | copy-start | bytes 786436
  498.8 5.2 %copy-start.6 = (f32[256,256]{1,0:T(8,128)}, f32[256,256]{1,0:T(8,128)S(1)}, u32[]{:S(2)}) copy-start(f32[256,256]{1,0:T(8,128)S(1)} %convolution_subtract_fusion.1) | copy-start | bytes 786436
  500.3 3.8 copy-start.7
Sparse Core Ops, SparseCore 0:
  50.1 22.3 all-gather.2
  87.2 22.3 all-gather.4
  113.2 118.7 reduce-scatter.2
  235.4 117.2 reduce-scatter.4
  366.3 130.8 all-reduce.2
where the time goes:
time: 511 us
  waiting for transfers between devices  348 us (68%)
  local copies, waits for them, and re-layouts  82.7 us (16%)
  matrix products  50.7 us (10%)
  between operations  14.1 us (3%)
  other arithmetic  10.7 us (2%)
    psum x1, waiting for transfers between devices, local(): lax.psum((partial_gram, partial_cross), ('row', 'col'))  129 us
    reduce_scatter x1, waiting for transfers between devices, local(): lax.psum_scatter(product_term(ancestor_inverse, gathered_two, place(gathe...  120 us
    reduce_scatter x1, waiting for transfers between devices, local(): lax.psum_scatter(product_term(ancestor_inverse, gathered_one, place(gathe...  96 us
    dot_general x5, matrix products, contract_rows(): lax.dot_general(left, right, (((0,), (0,)), ((), ())), precision=lax.Prec...  42.4 us
    scatter x1, local copies, waits for them, and re-layouts, local(): mask_one = jnp.zeros((ANC,), jnp.float32).at[struct_one].set(1.0)  39.8 us
    scatter x1, local copies, waits for them, and re-layouts, local(): mask_two = jnp.zeros((ANC,), jnp.float32).at[struct_two].set(1.0)  34.2 us
  transfers between devices with their start and end apart: 6, of which 4 were waited for; matrix products, arithmetic and copies ran while one was open for 17% of the time, Pallas kernels for 0%

commit v1 on v0

v1 whole, which is shorter than its diff:
```python
import jax
import jax.numpy as jnp
from jax import lax
from jax.sharding import PartitionSpec as P

CAP = 2


def matmul(left, right):
    return jnp.dot(left, right, precision=lax.Precision.HIGHEST, preferred_element_type=jnp.float32)


def contract_rows(left, right, precision=lax.Precision.HIGHEST):
    return lax.dot_general(
        left,
        right,
        (((0,), (0,)), ((), ())),
        precision=precision,
        preferred_element_type=jnp.float32,
    )


def row_mask(struct, count):
    lanes = 128
    high = struct // lanes
    low = struct % lanes
    high_hot = (jnp.arange(count // lanes, dtype=jnp.int32)[:, None] == high[None, :]).astype(jnp.bfloat16)
    low_hot = (jnp.arange(lanes, dtype=jnp.int32)[:, None] == low[None, :]).astype(jnp.bfloat16)
    counts = lax.dot_general(high_hot, low_hot, (((1,), (1,)), ((), ())), preferred_element_type=jnp.float32)
    return (counts > 0.5).astype(jnp.float32).reshape(count)


def deliver(values, tile_owner, col_count):
    tile_count = tile_owner.shape[0]
    tile_rows = values.shape[0] // tile_count
    all_tiles = values.reshape(tile_count, tile_rows, values.shape[1])
    owner_col = tile_owner[:, 0]
    col_ids = jnp.arange(col_count, dtype=jnp.int32)
    onehot = (owner_col[:, None] == col_ids[None, :]).astype(jnp.int32)
    tile_rank = jnp.sum((jnp.cumsum(onehot, axis=0) - onehot) * onehot, axis=1)
    slot_index = jnp.arange(CAP, dtype=jnp.int32)
    select = (
        (owner_col[None, None, :] == col_ids[:, None, None])
        & (tile_rank[None, None, :] == slot_index[None, :, None])
    ).astype(jnp.float32)
    outgoing = jnp.einsum("cks,srb->ckrb", select, all_tiles, precision=lax.Precision.HIGHEST)
    incoming = lax.all_to_all(outgoing, "col", split_axis=0, concat_axis=0, tiled=True)
    return incoming.reshape(col_count * CAP, tile_rows, values.shape[1])


def local(
    ancestor_inverse,
    panel_one,
    struct_one,
    lower_one,
    panel_two,
    struct_two,
    panel_above,
    lower_two,
    tile_owner,
):
    row_count = lax.axis_size("row")
    col_count = lax.axis_size("col")
    row_index = lax.axis_index("row")
    col_index = lax.axis_index("col")
    local_rows = panel_one.shape[0]
    order = local_rows * row_count * col_count
    width = panel_one.shape[1]
    mask_one = row_mask(struct_one, order)
    mask_two = row_mask(struct_two, order)
    panel_start = (row_index * col_count + col_index) * local_rows
    result_start = (col_index * row_count + row_index) * local_rows
    local_one = panel_one * lax.dynamic_slice_in_dim(mask_one, panel_start, local_rows)[:, None]
    local_two = panel_two * lax.dynamic_slice_in_dim(mask_two, panel_start, local_rows)[:, None]
    result_mask_one = lax.dynamic_slice_in_dim(mask_one, result_start, local_rows)[:, None]
    result_mask_two = lax.dynamic_slice_in_dim(mask_two, result_start, local_rows)[:, None]

    both = jnp.concatenate([local_one, local_two], axis=1)
    gathered = lax.all_gather(both, "col", axis=0, tiled=True)
    moves = [(f, (f % row_count) * col_count + f // row_count) for f in range(row_count * col_count)]
    resident = lax.ppermute(both, ("row", "col"), moves)
    product = lax.psum_scatter(
        contract_rows(ancestor_inverse, gathered, lax.Precision.HIGH),
        "row",
        scatter_dimension=0,
        tiled=True,
    )
    resident_one = resident[:, :width]
    resident_two = resident[:, width:]
    inverse_one = -product[:, :width] * result_mask_one
    inverse_two = -(product[:, width:] + matmul(inverse_one, panel_above)) * result_mask_two
    sums = lax.psum(
        jnp.concatenate(
            [
                contract_rows(resident_one, inverse_one),
                contract_rows(inverse_one, resident_two),
                contract_rows(resident_two, inverse_two),
            ],
            axis=1,
        ),
        ("row", "col"),
    )
    gram_one = sums[:, :width]
    cross_sum = sums[:, width : 2 * width]
    gram_two = sums[:, 2 * width :]
    diag_one = matmul(lower_one.T, lower_one) - gram_one
    cross_two = -(cross_sum + matmul(diag_one, panel_above))
    diag_two = matmul(lower_two.T, lower_two) - gram_two - matmul(panel_above.T, cross_two)
    delivered = deliver(inverse_two, tile_owner, col_count)
    return (inverse_one, diag_one, cross_two, diag_two, delivered)


def solution(mesh):
    return jax.shard_map(
        local,
        mesh=mesh,
        in_specs=(
            P("row", "col"),
            P(("row", "col"), None),
            P(),
            P(),
            P(("row", "col"), None),
            P(),
            P(),
            P(),
            P(("col", "row"), None),
        ),
        out_specs=(P(("col", "row"), None), P(), P(), P(), P(("row", "col"), None, None)),
        check_vma=False,
    )
```

time: 511 us -> 392 us (0.77)
  local copies, waits for them, and re-layouts: 82.7 us -> 4 us
  waiting for transfers between devices: 348 us -> 329 us
  matrix products: 50.7 us -> 35.3 us
  other arithmetic: 10.7 us -> 5.13 us
    scatter x2 -> x0, local copies, waits for them, and re-layouts: 74 us -> none  [the longest x1 39.8 us: local(): mask_one = jnp.zeros((ANC,), jnp.float32).at[struct_one].set(1.0)]
    reduce_scatter x2 -> x1, waiting for transfers between devices: 216 us -> 166 us  [local(): lax.psum_scatter(contract_rows(ancestor_inverse, gathered, lax.Precision....]
    all_gather x2 -> x1, waiting for transfers between devices: 0.04 us -> 31.3 us  [local(): gathered = lax.all_gather(both, 'col', axis=0, tiled=True)]
    dot_general x5 -> x6, matrix products: 42.4 us -> 27.1 us  [the longest x4 24.4 us: contract_rows(): lax.dot_general(left, right, (((0,), (0,)), ((), ())), precision=precisio...]
  transfers between devices with their start and end apart: 6 -> 5, of which waited for: 4 -> 4; matrix products, arithmetic and copies ran while one was open for 17% -> 2% of each run, Pallas kernels for 0% -> 0%
where the time goes in v1:
time: 392 us
  waiting for transfers between devices  329 us (84%)
  matrix products  35.3 us (9%)
  between operations  14 us (4%)
  other arithmetic  5.13 us (1%)
  starting transfers between devices  4.47 us (1%)
  local copies, waits for them, and re-layouts  4 us (1%)
    reduce_scatter x1, waiting for transfers between devices, local(): lax.psum_scatter(contract_rows(ancestor_inverse, gathered, lax.Precision....  166 us
    psum x1, waiting for transfers between devices, local(): lax.psum(jnp.concatenate([contract_rows(resident_one, inverse_one), contr...  127 us
    all_gather x1, waiting for transfers between devices, local(): gathered = lax.all_gather(both, 'col', axis=0, tiled=True)  31.3 us
    dot_general x4, matrix products, contract_rows(): lax.dot_general(left, right, (((0,), (0,)), ((), ())), precision=precisio...  24.4 us
  transfers between devices with their start and end apart: 5, of which 4 were waited for; matrix products, arithmetic and copies ran while one was open for 2% of the time, Pallas kernels for 0%

profile of v1, /device:TPU:0, one launch (start us, length us, event | category | flops | bytes accessed | tf_op | source)
XLA Modules:
  0.0 391.7 jit_solution(2987590773812136722)
XLA Ops:
  7.3 0.9 add_select_fusion.1
  8.2 0.8 add_select_fusion.3
  9.0 1.4 fusion.15
  10.4 1.3 fusion.12
  11.8 0.1 broadcast_multiply_fusion
  11.9 0.1 broadcast_multiply_fusion.1
  12.0 1.0 pad_maximum_fusion
  13.1 31.3 %all-gather.2.cloned.1.call-done = f32[1536,512]{1,0:T(8,128)} async-done(((f32[384,512]{1,0:T(8,128)}), f32[1536,512]{1,0:T(8,128)}) %all-gather.2.cloned.1.call-update) | async-done | bytes 3145744 | tf_op jit(solution)/shard_map/all_gather | solution.py:79
  44.4 22.2 %convolution_bitcast_fusion = f32[3072,512]{0,1:T(8,128)} fusion(f32[1536,512]{1,0:T(8,128)} %all-gather.2.cloned.1.call-done, f32[1536,3072]{1,0:T(8,128)} %param.9), kind=kOutput, calls=%fused_computation.2 | convolution fusion | flops 14495514624 | bytes 28311552 | tf_op jit(solution)/shard_map/dot_general | solution.py:14
  66.6 1.1 copy-done.1
  67.7 0.7 collective-permute-start
  68.5 0.2 reduce_window_sum.11
  68.7 166.1 %reduce-scatter.2.cloned.1.call-done = f32[384,512]{0,1:T(8,128)} async-done(((f32[3072,512]{0,1:T(8,128)}), f32[384,512]{0,1:T(8,128)}) %reduce-scatter.2.cloned.1.call-update) | async-done | bytes 786448 | tf_op jit(solution)/shard_map/reduce_scatter | solution.py:82
  234.8 1.0 fusion.21
  235.9 1.6 fusion.7
  237.5 0.2 copy.44
  237.7 0.7 fusion.16
  238.4 0.9 copy.46
  239.2 3.5 all-to-all-start
  242.7 0.2 all-reduce.2.cloned.1.call-start
  243.0 0.8 fusion.19
  243.8 0.6 fusion.24
  244.4 0.8 fusion.22
  245.2 1.0 pad_maximum_fusion.1
  246.2 0.9 copy.47
  247.1 4.4 %all-to-all-done = f32[4,2,64,256]{3,2,1,0:T(8,128)S(1)} async-done(((f32[4,2,64,256]{3,2,1,0:T(8,128)}), f32[4,2,64,256]{3,2,1,0:T(8,128)S(1)}, u32[]{:S(2)}, u32[]{:S(2)}) %all-to-all-start) | async-done | bytes 524320 | tf_op jit(solution)/shard_map/all_to_all | solution.py:47
  251.5 126.9 %all-reduce.2.cloned.1.call-done = f32[256,768]{1,0:T(8,128)} async-done(((f32[256,768]{1,0:T(8,128)}), f32[256,768]{1,0:T(8,128)}) %all-reduce.2.cloned.1.call-update) | async-done | bytes 786448 | tf_op jit(solution)/shard_map/psum | solution.py:92
  378.4 1.5 convolution_subtract_fusion.1
  379.9 1.4 fusion.9
  381.4 1.6 convolution_subtract_fusion
  383.0 1.3 fusion.8
  384.3 0.8 copy.60
  (28 shorter events, 0.3 us)
Async XLA Ops:
  7.2 228.7 %copy-start = (f32[256,256]{1,0:T(8,128)S(1)}, f32[256,256]{1,0:T(8,128)}, u32[]{:S(2)}) copy-start(f32[256,256]{1,0:T(8,128)} %param.15) | copy-start | bytes 786436
  7.2 4.6 %copy-start.6 = (f32[384,256]{1,0:T(8,128)S(1)}, f32[384,256]{1,0:T(8,128)}, u32[]{:S(2)}) copy-start(f32[384,256]{1,0:T(8,128)} %param.13) | copy-start | bytes 1179652
  7.2 4.7 %copy-start.7 = (f32[384,256]{1,0:T(8,128)S(1)}, f32[384,256]{1,0:T(8,128)}, u32[]{:S(2)}) copy-start(f32[384,256]{1,0:T(8,128)} %param.10) | copy-start | bytes 1179652
  7.2 37.2 %all-gather.2.cloned.1.call-start = ((), (), s32[]{:S(2)}) async-start(), calls=%async_computation.2 | async-start | bytes 3932160 | tf_op jit(solution)/shard_map/all_gather | solution.py:79
  13.0 221.8 %reduce-scatter.2.cloned.1.call-start = ((), (), s32[]{:S(2)}) async-start(), calls=%async_computation.3 | async-start | bytes 7077888 | tf_op jit(solution)/shard_map/reduce_scatter | solution.py:82
  66.6 1.1 copy-start.1
  66.6 1.8 copy-start.8
  67.7 175.2 %collective-permute-start = (f32[384,512]{1,0:T(8,128)S(1)}, f32[384,512]{1,0:T(8,128)S(1)}, u32[]{:S(2)}, u32[]{:S(2)}) collective-permute-start(f32[384,512]{1,0:T(8,128)S(1)} %copy-done.1), channel_id=1, source_target_pairs={{0,0},{1,4},{2,8},{3,12},{4,16},{5,20},{6,24},{7,28},{8,1},{9,5},{... | collective-permute-start | bytes 2359304 | tf_op jit(solution)/shard_map/ppermute | solution.py:81
  238.3 140.0 %copy-start.2 = (f32[256,256]{1,0:T(8,128)S(1)}, f32[256,256]{1,0:T(8,128)}, u32[]{:S(2)}) copy-start(f32[256,256]{1,0:T(8,128)} %param.12) | copy-start | bytes 786436
  239.2 12.3 %all-to-all-start = ((f32[4,2,64,256]{3,2,1,0:T(8,128)}), f32[4,2,64,256]{3,2,1,0:T(8,128)S(1)}, u32[]{:S(2)}, u32[]{:S(2)}) async-start(f32[4,2,64,256]{3,2,1,0:T(8,128)} %copy.46), calls=%async_computation.1 | async-start | bytes 1048576 | tf_op jit(solution)/shard_map/all_to_all | solution.py:47
  242.7 135.6 %all-reduce.2.cloned.1.call-start = ((), (), s32[]{:S(2)}) async-start(), calls=%async_computation.4 | async-start | bytes 1572864 | tf_op jit(solution)/shard_map/psum | solution.py:92
  243.0 138.4 %copy-start.3 = (f32[256,256]{1,0:T(8,128)S(1)}, f32[256,256]{1,0:T(8,128)}, u32[]{:S(2)}) copy-start(f32[256,256]{1,0:T(8,128)} %param.16) | copy-start | bytes 786436
  379.9 5.2 %copy-start.4 = (f32[256,256]{1,0:T(8,128)}, f32[256,256]{1,0:T(8,128)S(1)}, u32[]{:S(2)}) copy-start(f32[256,256]{1,0:T(8,128)S(1)} %convolution_subtract_fusion.1) | copy-start | bytes 786436
  381.4 3.8 copy-start.5
Sparse Core Ops, SparseCore 0:
  13.2 31.2 all-gather.1
  66.7 168.0 reduce-scatter.1
  248.7 129.5 all-reduce.1

commit v2 on v1

--- a/solution.py
+++ b/solution.py
@@ -1,6 +1,10 @@
+import functools
+
 import jax
 import jax.numpy as jnp
 from jax import lax
+from jax.experimental import pallas as pl
+from jax.experimental.pallas import tpu as pltpu
 from jax.sharding import PartitionSpec as P
 
 CAP = 2
@@ -28,6 +32,194 @@
     low_hot = (jnp.arange(lanes, dtype=jnp.int32)[:, None] == low[None, :]).astype(jnp.bfloat16)
     counts = lax.dot_general(high_hot, low_hot, (((1,), (1,)), ((), ())), preferred_element_type=jnp.float32)
     return (counts > 0.5).astype(jnp.float32).reshape(count)
+
+
+MESH = pl.DeviceIdType.MESH
+
+
+def greet(peers):
+    barrier = pltpu.get_barrier_semaphore()
+    for peer in peers:
+        pl.semaphore_signal(barrier, inc=1, device_id=peer, device_id_type=MESH)
+    pl.semaphore_wait(barrier, len(peers))
+
+
+def scatter_kernel(rows, value_ref, out_ref, pair_in, total, major_in, pair_send, pair_recv, major_send, major_recv):
+    majors = rows // 2
+    row = lax.axis_index("row")
+    col = lax.axis_index("col")
+    major, minor = row // 2, row % 2
+    partner = (major * 2 + 1 - minor, col)
+
+    def peer(offset):
+        return (lax.rem(major + offset, majors) * 2 + minor, col)
+
+    greet([partner] + [peer(offset) for offset in range(1, majors)])
+    order = sorted(range(1, majors), key=lambda offset: -min(offset, majors - offset)) + [0]
+    started = []
+    pair_copies = {}
+    for offset in order:
+        target = lax.rem(major + offset, majors)
+        copy = pltpu.make_async_remote_copy(
+            src_ref=value_ref.at[target * 2 + 1 - minor],
+            dst_ref=pair_in.at[offset],
+            send_sem=pair_send.at[offset],
+            recv_sem=pair_recv.at[offset],
+            device_id=partner,
+            device_id_type=MESH,
+        )
+        copy.start()
+        pair_copies[offset] = copy
+    for offset in order:
+        target = lax.rem(major + offset, majors)
+        pair_copies[offset].wait_recv()
+        total[offset] = pair_in[offset] + value_ref[target * 2 + minor]
+        if offset:
+            copy = pltpu.make_async_remote_copy(
+                src_ref=total.at[offset],
+                dst_ref=major_in.at[offset - 1],
+                send_sem=major_send.at[offset - 1],
+                recv_sem=major_recv.at[offset - 1],
+                device_id=peer(offset),
+                device_id_type=MESH,
+            )
+            copy.start()
+            started.append(copy)
+    for copy in started:
+        copy.wait_recv()
+    result = total[0]
+    for slot in range(majors - 1):
+        result = result + major_in[slot]
+    out_ref[...] = result
+    for copy in started:
+        copy.wait_send()
+    for offset in order:
+        pair_copies[offset].wait_send()
+
+
+def scatter_rows(value, rows):
+    chunk, width = value.shape[0] // rows, value.shape[1]
+    majors = rows // 2
+    dma = pltpu.SemaphoreType.DMA
+    return pl.pallas_call(
+        functools.partial(scatter_kernel, rows),
+        out_shape=jax.ShapeDtypeStruct((chunk, width), jnp.float32),
+        in_specs=[pl.BlockSpec(memory_space=pltpu.VMEM)],
+        out_specs=pl.BlockSpec(memory_space=pltpu.VMEM),
+        scratch_shapes=[
+            pltpu.VMEM((majors, chunk, width), jnp.float32),
+            pltpu.VMEM((majors, chunk, width), jnp.float32),
+            pltpu.VMEM((majors - 1, chunk, width), jnp.float32),
+            dma((majors,)),
+            dma((majors,)),
+            dma((majors - 1,)),
+            dma((majors - 1,)),
+        ],
+        compiler_params=pltpu.CompilerParams(
+            collective_id=0, has_side_effects=True, vmem_limit_bytes=40 * 2**20
+        ),
+    )(value.reshape(rows, chunk, width))
+
+
+def sum_kernel(rows, cols, value_ref, out_ref, full, sum_a, sum_b, in_a, in_b, in_c, *sems):
+    row = lax.axis_index("row")
+    col = lax.axis_index("col")
+    outer = cols // 2
+    far, core = col // 2, col % 2
+    half = outer * rows
+    base_a = core * half
+    base_b = base_a + far * rows
+    base_c = base_b + row
+
+    def pair_peer(offset):
+        return (row, far * 2 + 1 - core)
+
+    def far_peer(offset):
+        return (row, lax.rem(far + offset, outer) * 2 + core)
+
+    def row_peer(offset):
+        return (lax.rem(row + offset, rows), col)
+
+    greet(
+        [pair_peer(1)]
+        + [far_peer(offset) for offset in range(1, outer)]
+        + [row_peer(offset) for offset in range(1, rows)]
+    )
+
+    def exchange(count, peer, source, landing, stage):
+        copies = []
+        for offset in range(1, count):
+            copy = pltpu.make_async_remote_copy(
+                src_ref=source(offset),
+                dst_ref=landing(offset),
+                send_sem=sems[2 * stage].at[offset - 1],
+                recv_sem=sems[2 * stage + 1].at[offset - 1],
+                device_id=peer(offset),
+                device_id_type=MESH,
+            )
+            copy.start()
+            copies.append(copy)
+        for copy in copies:
+            copy.wait_recv()
+        return copies
+
+    pending = []
+    pending += exchange(
+        2, pair_peer, lambda k: value_ref.at[pl.ds((1 - core) * half, half)], lambda k: in_a.at[k - 1], 0
+    )
+    sum_a[...] = value_ref[pl.ds(base_a, half)] + in_a[0]
+    pending += exchange(
+        outer, far_peer, lambda k: sum_a.at[pl.ds(lax.rem(far + k, outer) * rows, rows)], lambda k: in_b.at[k - 1], 1
+    )
+    total = sum_a[pl.ds(far * rows, rows)]
+    for slot in range(outer - 1):
+        total = total + in_b[slot]
+    sum_b[...] = total
+    pending += exchange(
+        rows, row_peer, lambda k: sum_b.at[lax.rem(row + k, rows)], lambda k: in_c.at[k - 1], 2
+    )
+    total = sum_b[row]
+    for slot in range(rows - 1):
+        total = total + in_c[slot]
+    full[base_c] = total
+    pending += exchange(rows, row_peer, lambda k: full.at[base_c], lambda k: full.at[base_c], 3)
+    pending += exchange(
+        outer, far_peer, lambda k: full.at[pl.ds(base_b, rows)], lambda k: full.at[pl.ds(base_b, rows)], 4
+    )
+    pending += exchange(
+        2, pair_peer, lambda k: full.at[pl.ds(base_a, half)], lambda k: full.at[pl.ds(base_a, half)], 5
+    )
+    out_ref[...] = full[...]
+    for copy in pending:
+        copy.wait_send()
+
+
+def sum_everywhere(value, rows, cols):
+    devices = rows * cols
+    lanes = value.shape[1]
+    depth = value.shape[0] // devices
+    outer = cols // 2
+    dma = pltpu.SemaphoreType.DMA
+    vmem = lambda *lead: pltpu.VMEM(lead + (depth, lanes), jnp.float32)
+    total = pl.pallas_call(
+        functools.partial(sum_kernel, rows, cols),
+        out_shape=jax.ShapeDtypeStruct((devices, depth, lanes), jnp.float32),
+        in_specs=[pl.BlockSpec(memory_space=pltpu.VMEM)],
+        out_specs=pl.BlockSpec(memory_space=pltpu.VMEM),
+        scratch_shapes=[
+            vmem(devices),
+            vmem(devices // 2),
+            vmem(rows),
+            vmem(1, devices // 2),
+            vmem(outer - 1, rows),
+            vmem(rows - 1),
+        ]
+        + [dma((count - 1,)) for count in (2, outer, rows, rows, outer, 2) for _ in range(2)],
+        compiler_params=pltpu.CompilerParams(
+            collective_id=1, has_side_effects=True, vmem_limit_bytes=24 * 2**20
+        ),
+    )(value.reshape(devices, depth, lanes))
+    return total.reshape(value.shape)
 
 
 def deliver(values, tile_owner, col_count):
@@ -79,30 +271,24 @@
     gathered = lax.all_gather(both, "col", axis=0, tiled=True)
     moves = [(f, (f % row_count) * col_count + f // row_count) for f in range(row_count * col_count)]
     resident = lax.ppermute(both, ("row", "col"), moves)
-    product = lax.psum_scatter(
-        contract_rows(ancestor_inverse, gathered, lax.Precision.HIGH),
-        "row",
-        scatter_dimension=0,
-        tiled=True,
-    )
+    product = scatter_rows(contract_rows(ancestor_inverse, gathered, lax.Precision.HIGH), row_count)
     resident_one = resident[:, :width]
     resident_two = resident[:, width:]
     inverse_one = -product[:, :width] * result_mask_one
     inverse_two = -(product[:, width:] + matmul(inverse_one, panel_above)) * result_mask_two
-    sums = lax.psum(
-        jnp.concatenate(
-            [
-                contract_rows(resident_one, inverse_one),
-                contract_rows(inverse_one, resident_two),
-                contract_rows(resident_two, inverse_two),
-            ],
-            axis=1,
-        ),
-        ("row", "col"),
-    )
-    gram_one = sums[:, :width]
-    cross_sum = sums[:, width : 2 * width]
-    gram_two = sums[:, 2 * width :]
+    grams = (
+        contract_rows(resident_one, inverse_one),
+        contract_rows(inverse_one, resident_two),
+        contract_rows(resident_two, inverse_two),
+    )
+    lanes = 128
+    packed = jnp.concatenate(
+        [gram[:, at : at + lanes] for gram in grams for at in range(0, width, lanes)], axis=0
+    )
+    sums = sum_everywhere(packed, row_count, col_count).reshape(len(grams), width // lanes, width, lanes)
+    gram_one, cross_sum, gram_two = (
+        jnp.concatenate([sums[at, block] for block in range(width // lanes)], axis=1) for at in range(len(grams))
+    )
     diag_one = matmul(lower_one.T, lower_one) - gram_one
     cross_two = -(cross_sum + matmul(diag_one, panel_above))
     diag_two = matmul(lower_two.T, lower_two) - gram_two - matmul(panel_above.T, cross_two)

time: 392 us -> 249 us (0.64)
  waiting for transfers between devices: 329 us -> 62.6 us
  Pallas kernels: 0 us -> 120 us
  local copies, waits for them, and re-layouts: 4 us -> 11.3 us
    reduce_scatter x1 -> x0, waiting for transfers between devices: 166 us -> none  [local(): lax.psum_scatter(contract_rows(ancestor_inverse, gathered, lax.Precision....]
    psum x1 -> x0, waiting for transfers between devices: 127 us -> none  [local(): lax.psum(jnp.concatenate([contract_rows(resident_one, inverse_one), contr...]
    pallas_call x0 -> x2, Pallas kernels: none -> 120 us  [the longest x1 92.6 us: scatter_rows(): pl.pallas_call(functools.partial(scatter_kernel, rows), out_shape=jax.Sha...]
    all_gather x1, waiting for transfers between devices: 31.3 us -> 56.7 us  [local(): gathered = lax.all_gather(both, 'col', axis=0, tiled=True)]
    dot_general x0 -> x1, local copies, waits for them, and re-layouts: none -> 6.55 us  [contract_rows(): lax.dot_general(left, right, (((0,), (0,)), ((), ())), precision=precisio...]
    dot_general x5, matrix products: 7.55 us -> 3.37 us  [matmul(): jnp.dot(left, right, precision=lax.Precision.HIGHEST, preferred_element_t...]
  transfers between devices with their start and end apart: 5 -> 3, of which waited for: 4 -> 2; matrix products, arithmetic and copies ran while one was open for 2% -> 13% of each run, Pallas kernels for 0% -> 37%
where the time goes in v2:
time: 249 us; the launch traced here: 248 us
  Pallas kernels  120 us (48%)
  waiting for transfers between devices  62.6 us (25%)
  matrix products  31.4 us (13%)
  between operations  14.3 us (6%)
  local copies, waits for them, and re-layouts  11.3 us (5%)
  starting transfers between devices  5.3 us (2%)
  other arithmetic  3.33 us (1%)
    pallas_call x1, Pallas kernels, scatter_rows(): pl.pallas_call(functools.partial(scatter_kernel, rows), out_shape=jax.Sha...  92.6 us
    all_gather x1, waiting for transfers between devices, local(): gathered = lax.all_gather(both, 'col', axis=0, tiled=True)  56.7 us
    pallas_call x1, Pallas kernels, sum_everywhere(): pl.pallas_call(functools.partial(sum_kernel, rows, cols), out_shape=jax.S...  27.3 us
    dot_general x4, matrix products, contract_rows(): lax.dot_general(left, right, (((0,), (0,)), ((), ())), precision=precisio...  24.6 us
    dot_general x1, local copies, waits for them, and re-layouts, contract_rows(): lax.dot_general(left, right, (((0,), (0,)), ((), ())), precision=precisio...  6.55 us
    all_to_all x1, waiting for transfers between devices, deliver(): lax.all_to_all(outgoing, 'col', split_axis=0, concat_axis=0, tiled=True)  5.83 us
  transfers between devices with their start and end apart: 3, of which 2 were waited for; matrix products, arithmetic and copies ran while one was open for 13% of the time, Pallas kernels for 37%

profile of v2, /device:TPU:0, one launch (start us, length us, event | category | flops | bytes accessed | tf_op | source)
XLA Modules:
  0.0 248.1 jit_solution(17450690968271084024)
XLA Ops:
  7.2 0.0 all-gather.2.cloned.1.call-start
  7.3 0.9 add_select_fusion.1
  8.2 0.8 add_select_fusion.3
  9.0 1.4 fusion.15
  10.4 1.3 fusion.12
  11.7 0.1 fusion.34
  11.8 0.1 broadcast_multiply_fusion
  11.9 0.1 broadcast_multiply_fusion.1
  12.0 1.1 pad_maximum_fusion
  13.1 1.8 collective-permute-start
  14.9 0.2 reduce_window_sum.11
  15.1 56.7 %all-gather.2.cloned.1.call-done = f32[1536,512]{1,0:T(8,128)} async-done(((f32[384,512]{1,0:T(8,128)}), f32[1536,512]{1,0:T(8,128)}) %all-gather.2.cloned.1.call-update) | async-done | bytes 3145744 | tf_op jit(solution)/shard_map/all_gather | solution.py:271
  71.9 22.2 %convolution_bitcast_fusion = f32[3072,512]{0,1:T(8,128)} fusion(f32[1536,512]{1,0:T(8,128)} %all-gather.2.cloned.1.call-done, f32[1536,3072]{1,0:T(8,128)} %param.9), kind=kOutput, calls=%fused_computation.2 | convolution fusion | flops 14495514624 | bytes 28311552 | tf_op jit(solution)/shard_map/dot_general | solution.py:18
  94.0 6.6 %copy.25 = f32[3072,512]{1,0:T(8,128)} copy(f32[3072,512]{0,1:T(8,128)} %convolution_bitcast_fusion) | data formatting | bytes 12582912 | tf_op jit(solution)/shard_map/dot_general | solution.py:18
  100.6 2.8 %copy-done.1 = f32[3072,512]{1,0:T(8,128)S(1)} copy-done((f32[3072,512]{1,0:T(8,128)S(1)}, f32[3072,512]{1,0:T(8,128)}, u32[]{:S(2)}) %copy-start.1) | copy-done | bytes 6291480
  103.3 92.6 %shard_map.128 = f32[384,512]{1,0:T(8,128)S(1)} custom-call(f32[8,384,512]{2,1,0:T(8,128)S(1)} %bitcast.51), custom_call_target="tpu_custom_call" | custom-call | tf_op jit(solution)/shard_map/pallas_call | solution.py:104
  196.0 0.1 negate_multiply_fusion
  196.1 0.8 fusion.19
  197.0 0.8 fusion.23
  197.9 0.5 fusion.7
  198.4 0.8 fusion.21
  199.3 27.3 %shard_map.129 = f32[32,48,128]{2,1,0:T(8,128)S(1)} custom-call(f32[32,48,128]{2,1,0:T(8,128)S(1)} %bitcast.53), custom_call_target="tpu_custom_call" | custom-call | tf_op jit(solution)/shard_map/pallas_call | solution.py:204
  226.6 0.1 slice_bitcast_fusion.1
  226.7 0.7 fusion.16
  227.4 0.9 copy.28
  228.2 3.5 %all-to-all-start = ((f32[4,2,64,256]{3,2,1,0:T(8,128)}), f32[4,2,64,256]{3,2,1,0:T(8,128)S(1)}, u32[]{:S(2)}, u32[]{:S(2)}) async-start(f32[4,2,64,256]{3,2,1,0:T(8,128)} %copy.28), calls=%async_computation | async-start | bytes 1048576 | tf_op jit(solution)/shard_map/all_to_all | solution.py:239
  231.7 0.6 convolution_subtract_fusion
  232.3 0.6 convolution_subtract_fusion.1
  233.0 0.4 fusion.9
  233.4 1.3 fusion.8
  234.7 5.8 %all-to-all-done = f32[4,2,64,256]{3,2,1,0:T(8,128)S(1)} async-done(((f32[4,2,64,256]{3,2,1,0:T(8,128)}), f32[4,2,64,256]{3,2,1,0:T(8,128)S(1)}, u32[]{:S(2)}, u32[]{:S(2)}) %all-to-all-start) | async-done | bytes 524320 | tf_op jit(solution)/shard_map/all_to_all | solution.py:239
  240.5 0.8 copy.41
  (31 shorter events, 0.2 us)
Async XLA Ops:
  7.2 190.7 %copy-start = (f32[256,256]{1,0:T(8,128)S(1)}, f32[256,256]{1,0:T(8,128)}, u32[]{:S(2)}) copy-start(f32[256,256]{1,0:T(8,128)} %param.15) | copy-start | bytes 786436
  7.2 4.6 %copy-start.7 = (f32[384,256]{1,0:T(8,128)S(1)}, f32[384,256]{1,0:T(8,128)}, u32[]{:S(2)}) copy-start(f32[384,256]{1,0:T(8,128)} %param.13) | copy-start | bytes 1179652
  7.2 4.7 %copy-start.8 = (f32[384,256]{1,0:T(8,128)S(1)}, f32[384,256]{1,0:T(8,128)}, u32[]{:S(2)}) copy-start(f32[384,256]{1,0:T(8,128)} %param.10) | copy-start | bytes 1179652
  7.2 64.7 %all-gather.2.cloned.1.call-start = ((), (), s32[]{:S(2)}) async-start(), calls=%async_computation.1 | async-start | bytes 3932160 | tf_op jit(solution)/shard_map/all_gather | solution.py:271
  10.4 4.5 %copy-start.9 = (s32[6,1]{0,1:T(1,128)S(1)}, s32[6,1]{0,1:T(1,128)}, u32[]{:S(2)}) copy-start(s32[6,1]{0,1:T(1,128)} %param.17) | copy-start | bytes 76
  13.1 183.0 %collective-permute-start = (f32[384,512]{1,0:T(8,128)}, f32[384,512]{1,0:T(8,128)S(1)}, u32[]{:S(2)}, u32[]{:S(2)}) collective-permute-start(f32[384,512]{1,0:T(8,128)} %pad_maximum_fusion), channel_id=1, source_target_pairs={{0,0},{1,4},{2,8},{3,12},{4,16},{5,20},{6,24},{7,28},{8,1},{9,5},{... | collective-permute-start | bytes 2359304 | tf_op jit(solution)/shard_map/ppermute | solution.py:273
  100.6 2.8 %copy-start.1 = (f32[3072,512]{1,0:T(8,128)S(1)}, f32[3072,512]{1,0:T(8,128)}, u32[]{:S(2)}) copy-start(f32[3072,512]{1,0:T(8,128)} %copy.25) | copy-start | bytes 18874372
  196.1 30.6 %copy-start.2 = (f32[384,256]{1,0:T(8,128)}, f32[384,256]{1,0:T(8,128)S(1)}, u32[]{:S(2)}) copy-start(f32[384,256]{1,0:T(8,128)S(1)} %negate_multiply_fusion) | copy-start | bytes 1179652
  198.4 33.3 %copy-start.3 = (f32[256,256]{1,0:T(8,128)S(1)}, f32[256,256]{1,0:T(8,128)}, u32[]{:S(2)}) copy-start(f32[256,256]{1,0:T(8,128)} %param.16) | copy-start | bytes 786436
  199.2 33.1 %copy-start.4 = (f32[256,256]{1,0:T(8,128)S(1)}, f32[256,256]{1,0:T(8,128)}, u32[]{:S(2)}) copy-start(f32[256,256]{1,0:T(8,128)} %param.12) | copy-start | bytes 786436
  228.2 12.3 %all-to-all-start = ((f32[4,2,64,256]{3,2,1,0:T(8,128)}), f32[4,2,64,256]{3,2,1,0:T(8,128)S(1)}, u32[]{:S(2)}, u32[]{:S(2)}) async-start(f32[4,2,64,256]{3,2,1,0:T(8,128)} %copy.28), calls=%async_computation | async-start | bytes 1048576 | tf_op jit(solution)/shard_map/all_to_all | solution.py:239
  232.9 8.3 %copy-start.5 = (f32[256,256]{1,0:T(8,128)}, f32[256,256]{1,0:T(8,128)S(1)}, u32[]{:S(2)}) copy-start(f32[256,256]{1,0:T(8,128)S(1)} %convolution_subtract_fusion.1) | copy-start | bytes 786436
  233.4 7.9 %copy-start.6 = (f32[256,256]{1,0:T(8,128)}, f32[256,256]{1,0:T(8,128)S(1)}, u32[]{:S(2)}) copy-start(f32[256,256]{1,0:T(8,128)S(1)} %fusion.9) | copy-start | bytes 786436
Sparse Core Ops, SparseCore 0:
  13.2 58.5 all-gather.1

commit v3 on v2

--- a/solution.py
+++ b/solution.py
@@ -121,6 +121,201 @@
     )(value.reshape(rows, chunk, width))
 
 
+def gather_kernel(cols, parts, block_ref, high_ref, low_ref, held, pair_send, pair_recv, far_send, far_recv, relay_send, relay_recv):
+    row = lax.axis_index("row")
+    col = lax.axis_index("col")
+    outer = cols // 2
+    far, core = col // 2, col % 2
+    partner = (row, far * 2 + 1 - core)
+
+    def far_peer(offset):
+        return (row, lax.rem(far + offset, outer) * 2 + core)
+
+    greet([partner] + [far_peer(offset) for offset in range(1, outer)])
+
+    def send(source, slot, part, target, send_sem, recv_sem):
+        copy = pltpu.make_async_remote_copy(
+            src_ref=source,
+            dst_ref=held.at[slot, part],
+            send_sem=send_sem,
+            recv_sem=recv_sem,
+            device_id=target,
+            device_id_type=MESH,
+        )
+        copy.start()
+        return copy
+
+    far_copies = [
+        (offset, part, send(
+            block_ref.at[part], col, part, far_peer(offset), far_send.at[offset - 1, part], far_recv.at[offset - 1, part]
+        ))
+        for part in range(parts)
+        for offset in range(1, outer)
+    ]
+    pair_copies = [
+        send(block_ref.at[part], col, part, partner, pair_send.at[part], pair_recv.at[part]) for part in range(parts)
+    ]
+    relays = []
+    for offset, part, copy in far_copies:
+        copy.wait_recv()
+        source = lax.rem(far - offset + outer, outer) * 2 + core
+        relays.append(
+            send(
+                held.at[source, part],
+                source,
+                part,
+                partner,
+                relay_send.at[offset - 1, part],
+                relay_recv.at[offset - 1, part],
+            )
+        )
+    held[col] = block_ref[...]
+    for copy in pair_copies + relays:
+        copy.wait_recv()
+    height, length = block_ref.shape[1:]
+    for slot in range(cols):
+        for part in range(parts):
+            value = held[slot, part]
+            high = value.astype(jnp.bfloat16)
+            place = (pl.ds(part * height, height), pl.ds(slot * length, length))
+            high_ref[place] = high
+            low_ref[place] = (value - high.astype(jnp.float32)).astype(jnp.bfloat16)
+    for copy in pair_copies + relays + [entry[2] for entry in far_copies]:
+        copy.wait_send()
+
+
+def gather_columns(block, cols):
+    parts = 2
+    width, length = block.shape
+    outer = cols // 2
+    dma = pltpu.SemaphoreType.DMA
+    return pl.pallas_call(
+        functools.partial(gather_kernel, cols, parts),
+        out_shape=[jax.ShapeDtypeStruct((width, cols * length), jnp.bfloat16)] * 2,
+        in_specs=[pl.BlockSpec(memory_space=pltpu.VMEM)],
+        out_specs=[pl.BlockSpec(memory_space=pltpu.VMEM)] * 2,
+        scratch_shapes=[pltpu.VMEM((cols, parts, width // parts, length), jnp.float32)]
+        + [dma((parts,))] * 2
+        + [dma((outer - 1, parts))] * 4,
+        compiler_params=pltpu.CompilerParams(
+            collective_id=2, has_side_effects=True, vmem_limit_bytes=24 * 2**20
+        ),
+    )(block.reshape(parts, width // parts, length))
+
+
+def product_kernel(
+    rows, matrix_ref, high_ref, low_ref, out_ref, window, mine, other, pair_in, major_in,
+    window_sem, pair_send, pair_recv, major_send, major_recv,
+):
+    majors = rows // 2
+    row = lax.axis_index("row")
+    col = lax.axis_index("col")
+    major, minor = row // 2, row % 2
+    partner = (major * 2 + 1 - minor, col)
+    span = out_ref.shape[1]
+
+    def peer(offset):
+        return (lax.rem(major + offset, majors) * 2 + minor, col)
+
+    def fetch(step, which):
+        target = lax.rem(major + step + 1, majors) * 2 + lax.rem(1 - minor + which, 2)
+        return pltpu.make_async_copy(
+            matrix_ref.at[:, pl.ds(pl.multiple_of(target * span, 128), span)],
+            window.at[which],
+            window_sem.at[which],
+        )
+
+    def pair_copy(step):
+        return pltpu.make_async_remote_copy(
+            src_ref=other.at[step],
+            dst_ref=pair_in.at[step],
+            send_sem=pair_send.at[step],
+            recv_sem=pair_recv.at[step],
+            device_id=partner,
+            device_id_type=MESH,
+        )
+
+    for which in range(2):
+        fetch(0, which).start()
+    greet([partner] + [peer(offset) for offset in range(1, majors)])
+
+    def dot(left, right):
+        return jnp.dot(left, right, preferred_element_type=jnp.float32)
+
+    def body(step, carry):
+        for which, result in enumerate((other, mine)):
+            fetch(step, which).wait()
+            value = window[which]
+            high = value.astype(jnp.bfloat16)
+            low = (value - high.astype(jnp.float32)).astype(jnp.bfloat16)
+            result[step] = dot(high_ref[...], high) + (dot(high_ref[...], low) + dot(low_ref[...], high))
+
+            @pl.when(step + 1 < majors)
+            def _():
+                fetch(step + 1, which).start()
+
+            if which == 0:
+                pair_copy(step).start()
+        return carry
+
+    lax.fori_loop(0, majors, body, 0)
+    started = []
+    for step in range(majors):
+        pair_copy(step).wait_recv()
+        mine[step] = mine[step] + pair_in[step]
+        if step + 1 < majors:
+            copy = pltpu.make_async_remote_copy(
+                src_ref=mine.at[step],
+                dst_ref=major_in.at[step],
+                send_sem=major_send.at[step],
+                recv_sem=major_recv.at[step],
+                device_id=peer(step + 1),
+                device_id_type=MESH,
+            )
+            copy.start()
+            started.append(copy)
+    for copy in started:
+        copy.wait_recv()
+    result = mine[majors - 1]
+    for slot in range(majors - 1):
+        result = result + major_in[slot]
+    out_ref[...] = result
+    for copy in started:
+        copy.wait_send()
+    for step in range(majors):
+        pair_copy(step).wait_send()
+
+
+def product_rows(matrix, high, low, rows):
+    width = high.shape[0]
+    depth = matrix.shape[0]
+    span = matrix.shape[1] // rows
+    majors = rows // 2
+    dma = pltpu.SemaphoreType.DMA
+    vmem = lambda *shape: pltpu.VMEM(shape, jnp.float32)
+    return pl.pallas_call(
+        functools.partial(product_kernel, rows),
+        out_shape=jax.ShapeDtypeStruct((width, span), jnp.float32),
+        in_specs=[pl.BlockSpec(memory_space=pl.ANY)] + [pl.BlockSpec(memory_space=pltpu.VMEM)] * 2,
+        out_specs=pl.BlockSpec(memory_space=pltpu.VMEM),
+        scratch_shapes=[
+            vmem(2, depth, span),
+            vmem(majors, width, span),
+            vmem(majors, width, span),
+            vmem(majors, width, span),
+            vmem(majors - 1, width, span),
+            dma((2,)),
+            dma((majors,)),
+            dma((majors,)),
+            dma((majors - 1,)),
+            dma((majors - 1,)),
+        ],
+        compiler_params=pltpu.CompilerParams(
+            collective_id=0, has_side_effects=True, vmem_limit_bytes=48 * 2**20
+        ),
+    )(matrix, high, low)
+
+
 def sum_kernel(rows, cols, value_ref, out_ref, full, sum_a, sum_b, in_a, in_b, in_c, *sems):
     row = lax.axis_index("row")
     col = lax.axis_index("col")
@@ -268,10 +463,14 @@
     result_mask_two = lax.dynamic_slice_in_dim(mask_two, result_start, local_rows)[:, None]
 
     both = jnp.concatenate([local_one, local_two], axis=1)
-    gathered = lax.all_gather(both, "col", axis=0, tiled=True)
     moves = [(f, (f % row_count) * col_count + f // row_count) for f in range(row_count * col_count)]
     resident = lax.ppermute(both, ("row", "col"), moves)
-    product = scatter_rows(contract_rows(ancestor_inverse, gathered, lax.Precision.HIGH), row_count)
+    if local_rows % 128 == 0:
+        high, low = gather_columns(both.T, col_count)
+        product = product_rows(ancestor_inverse, high, low, row_count).T
+    else:
+        gathered = lax.all_gather(both, "col", axis=0, tiled=True)
+        product = scatter_rows(contract_rows(ancestor_inverse, gathered, lax.Precision.HIGH), row_count)
     resident_one = resident[:, :width]
     resident_two = resident[:, width:]
     inverse_one = -product[:, :width] * result_mask_one

time: 249 us -> 209 us (0.84)
  Pallas kernels: 120 us -> 181 us
  waiting for transfers between devices: 62.6 us -> 7.69 us
  matrix products: 31.4 us -> 9.07 us
  between operations: 14.3 us -> 0.98 us
  local copies, waits for them, and re-layouts: 11.3 us -> 3.28 us
    pallas_call x1 -> x2, Pallas kernels: 92.6 us -> 153 us  [the longest x1 96.1 us: product_rows(): pl.pallas_call(functools.partial(product_kernel, rows), out_shape=jax.Sha...]
    all_gather x1 -> x0, waiting for transfers between devices: 56.7 us -> none  [local(): gathered = lax.all_gather(both, 'col', axis=0, tiled=True)]
    dot_general x4 -> x3, matrix products: 24.6 us -> 2.19 us  [contract_rows(): lax.dot_general(left, right, (((0,), (0,)), ((), ())), precision=precisio...]
    dot_general x1 -> x0, local copies, waits for them, and re-layouts: 6.55 us -> none  [contract_rows(): lax.dot_general(left, right, (((0,), (0,)), ((), ())), precision=precisio...]
  transfers between devices with their start and end apart: 3 -> 2, of which waited for: 2 -> 1; matrix products, arithmetic and copies ran while one was open for 13% -> 2% of each run, Pallas kernels for 37% -> 74%
where the time goes in v3:
time: 209 us
  Pallas kernels  181 us (87%)
  matrix products  9.07 us (4%)
  waiting for transfers between devices  7.69 us (4%)
  starting transfers between devices  4.36 us (2%)
  local copies, waits for them, and re-layouts  3.28 us (2%)
  other arithmetic  2.4 us (1%)
    pallas_call x1, Pallas kernels, product_rows(): pl.pallas_call(functools.partial(product_kernel, rows), out_shape=jax.Sha...  96.1 us
    pallas_call x1, Pallas kernels, gather_columns(): pl.pallas_call(functools.partial(gather_kernel, cols, parts), out_shape=[...  57.4 us
    pallas_call x1, Pallas kernels, sum_everywhere(): pl.pallas_call(functools.partial(sum_kernel, rows, cols), out_shape=jax.S...  27.5 us
    all_to_all x1, waiting for transfers between devices, deliver(): lax.all_to_all(outgoing, 'col', split_axis=0, concat_axis=0, tiled=True)  7.68 us
  transfers between devices with their start and end apart: 2, of which 1 were waited for; matrix products, arithmetic and copies ran while one was open for 2% of the time, Pallas kernels for 74%

profile of v3, /device:TPU:0, one launch (start us, length us, event | category | flops | bytes accessed | tf_op | source)
XLA Modules:
  0.0 208.7 jit_solution(354799460115687641)
XLA Ops:
  0.6 0.0 copy-start
  0.7 0.9 add_select_fusion.1
  1.6 0.8 add_select_fusion.3
  2.4 1.4 fusion.15
  3.9 1.3 fusion.12
  5.1 0.1 fusion.36
  5.2 0.1 broadcast_multiply_fusion
  5.3 0.1 broadcast_multiply_fusion.1
  5.5 0.2 pad_maximum_fusion
  5.7 0.7 collective-permute-start
  6.4 0.3 copy.33
  6.7 57.4 %shard_map.128 = (bf16[512,1536]{1,0:T(8,128)(2,1)S(1)}, bf16[512,1536]{1,0:T(8,128)(2,1)S(1)}) custom-call(f32[2,256,384]{2,1,0:T(8,128)S(1)} %bitcast.53), custom_call_target="tpu_custom_call" | custom-call | tf_op jit(solution)/shard_map/pallas_call | solution.py:192
  64.1 96.1 %shard_map.129 = f32[512,384]{1,0:T(8,128)S(1)} custom-call(f32[1536,3072]{1,0:T(8,128)} %matrix_ref.1, bf16[512,1536]{1,0:T(8,128)(2,1)S(1)} %get-tuple-element.7.high_ref, bf16[512,1536]{1,0:T(8,128)(2,1)S(1)} %get-tuple-element.8.low_ref), custom_call_target="tpu_custom_call" | custom-call | tf_op jit(solution)/shard_map/pallas_call | solution.py:296
  160.2 0.6 fusion.7
  160.9 0.2 copy.36
  161.0 0.2 reduce_window_sum.11
  161.2 0.7 fusion.16
  161.9 0.9 copy.38
  162.8 3.7 %all-to-all-start = ((f32[4,2,64,256]{3,2,1,0:T(8,128)}), f32[4,2,64,256]{3,2,1,0:T(8,128)S(1)}, u32[]{:S(2)}, u32[]{:S(2)}) async-start(f32[4,2,64,256]{3,2,1,0:T(8,128)} %copy.38), calls=%async_computation | async-start | bytes 1048576 | tf_op jit(solution)/shard_map/all_to_all | solution.py:434
  166.5 0.9 copy.39
  167.4 7.7 %all-to-all-done = f32[4,2,64,256]{3,2,1,0:T(8,128)S(1)} async-done(((f32[4,2,64,256]{3,2,1,0:T(8,128)}), f32[4,2,64,256]{3,2,1,0:T(8,128)S(1)}, u32[]{:S(2)}, u32[]{:S(2)}) %all-to-all-start) | async-done | bytes 524320 | tf_op jit(solution)/shard_map/all_to_all | solution.py:434
  175.1 0.8 fusion.19
  176.0 0.6 fusion.24
  176.6 0.8 fusion.22
  177.4 27.5 %shard_map.130 = f32[32,48,128]{2,1,0:T(8,128)S(1)} custom-call(f32[32,48,128]{2,1,0:T(8,128)S(1)} %bitcast.54), custom_call_target="tpu_custom_call" | custom-call | tf_op jit(solution)/shard_map/pallas_call | solution.py:399
  204.9 0.1 slice_bitcast_fusion.1
  205.0 0.6 convolution_subtract_fusion
  205.6 0.6 convolution_subtract_fusion.1
  206.2 0.4 fusion.9
  206.6 0.0 copy-start.4
  206.6 1.3 fusion.8
  207.9 0.8 copy.53
  (26 shorter events, 0.2 us)
Async XLA Ops:
  0.6 159.6 %copy-start = (f32[256,256]{1,0:T(8,128)S(1)}, f32[256,256]{1,0:T(8,128)}, u32[]{:S(2)}) copy-start(f32[256,256]{1,0:T(8,128)} %param.15) | copy-start | bytes 786436
  0.6 4.6 %copy-start.5 = (f32[384,256]{1,0:T(8,128)S(1)}, f32[384,256]{1,0:T(8,128)}, u32[]{:S(2)}) copy-start(f32[384,256]{1,0:T(8,128)} %param.13) | copy-start | bytes 1179652
  0.7 4.7 %copy-start.6 = (f32[384,256]{1,0:T(8,128)S(1)}, f32[384,256]{1,0:T(8,128)}, u32[]{:S(2)}) copy-start(f32[384,256]{1,0:T(8,128)} %param.10) | copy-start | bytes 1179652
  3.8 2.5 %copy-start.7 = (s32[6,1]{0,1:T(1,128)S(1)}, s32[6,1]{0,1:T(1,128)}, u32[]{:S(2)}) copy-start(s32[6,1]{0,1:T(1,128)} %param.17) | copy-start | bytes 76
  5.7 169.4 %collective-permute-start = (f32[384,512]{1,0:T(8,128)S(1)}, f32[384,512]{1,0:T(8,128)S(1)}, u32[]{:S(2)}, u32[]{:S(2)}) collective-permute-start(f32[384,512]{1,0:T(8,128)S(1)} %get-tuple-element.35), channel_id=1, source_target_pairs={{0,0},{1,4},{2,8},{3,12},{4,16},{5,20},{6,24},{7,28},{8,1},{9,5},{... | collective-permute-start | bytes 2359304 | tf_op jit(solution)/shard_map/ppermute | solution.py:467
  162.8 12.3 %all-to-all-start = ((f32[4,2,64,256]{3,2,1,0:T(8,128)}), f32[4,2,64,256]{3,2,1,0:T(8,128)S(1)}, u32[]{:S(2)}, u32[]{:S(2)}) async-start(f32[4,2,64,256]{3,2,1,0:T(8,128)} %copy.38), calls=%async_computation | async-start | bytes 1048576 | tf_op jit(solution)/shard_map/all_to_all | solution.py:434
  175.9 29.1 %copy-start.1 = (f32[256,256]{1,0:T(8,128)S(1)}, f32[256,256]{1,0:T(8,128)}, u32[]{:S(2)}) copy-start(f32[256,256]{1,0:T(8,128)} %param.16) | copy-start | bytes 786436
  175.9 29.7 %copy-start.2 = (f32[256,256]{1,0:T(8,128)S(1)}, f32[256,256]{1,0:T(8,128)}, u32[]{:S(2)}) copy-start(f32[256,256]{1,0:T(8,128)} %param.12) | copy-start | bytes 786436
  206.2 2.5 %copy-start.3 = (f32[256,256]{1,0:T(8,128)}, f32[256,256]{1,0:T(8,128)S(1)}, u32[]{:S(2)}) copy-start(f32[256,256]{1,0:T(8,128)S(1)} %convolution_subtract_fusion.1) | copy-start | bytes 786436
  206.6 2.1 %copy-start.4 = (f32[256,256]{1,0:T(8,128)}, f32[256,256]{1,0:T(8,128)S(1)}, u32[]{:S(2)}) copy-start(f32[256,256]{1,0:T(8,128)S(1)} %fusion.9) | copy-start | bytes 786436

commit v4 on v3

--- a/solution.py
+++ b/solution.py
@@ -214,11 +214,14 @@
     partner = (major * 2 + 1 - minor, col)
     span = out_ref.shape[1]
 
-    def peer(offset):
-        return (lax.rem(major + offset, majors) * 2 + minor, col)
+    upper, lower = major // 2, major % 2
+    near = ((upper * 2 + 1 - lower) * 2 + minor, col)
+    away = (((1 - upper) * 2 + lower) * 2 + minor, col)
 
     def fetch(step, which):
-        target = lax.rem(major + step + 1, majors) * 2 + lax.rem(1 - minor + which, 2)
+        target_upper = lax.rem(upper + 1 + step // 2, 2)
+        target_lower = lax.rem(lower + 1 + step, 2)
+        target = (target_upper * 2 + target_lower) * 2 + lax.rem(1 - minor + which, 2)
         return pltpu.make_async_copy(
             matrix_ref.at[:, pl.ds(pl.multiple_of(target * span, 128), span)],
             window.at[which],
@@ -237,7 +240,7 @@
 
     for which in range(2):
         fetch(0, which).start()
-    greet([partner] + [peer(offset) for offset in range(1, majors)])
+    greet([partner, near, away])
 
     def dot(left, right):
         return jnp.dot(left, right, preferred_element_type=jnp.float32)
@@ -259,28 +262,36 @@
         return carry
 
     lax.fori_loop(0, majors, body, 0)
-    started = []
-    for step in range(majors):
-        pair_copy(step).wait_recv()
-        mine[step] = mine[step] + pair_in[step]
-        if step + 1 < majors:
-            copy = pltpu.make_async_remote_copy(
-                src_ref=mine.at[step],
-                dst_ref=major_in.at[step],
-                send_sem=major_send.at[step],
-                recv_sem=major_recv.at[step],
-                device_id=peer(step + 1),
-                device_id_type=MESH,
-            )
-            copy.start()
-            started.append(copy)
-    for copy in started:
-        copy.wait_recv()
-    result = mine[majors - 1]
-    for slot in range(majors - 1):
-        result = result + major_in[slot]
-    out_ref[...] = result
-    for copy in started:
+
+    def forward(source, slot, target):
+        copy = pltpu.make_async_remote_copy(
+            src_ref=mine.at[source],
+            dst_ref=major_in.at[slot],
+            send_sem=major_send.at[slot],
+            recv_sem=major_recv.at[slot],
+            device_id=target,
+            device_id_type=MESH,
+        )
+        copy.start()
+        return copy
+
+    pair_copy(0).wait_recv()
+    mine[0] = mine[0] + pair_in[0]
+    both_bits = forward(0, 0, near)
+    pair_copy(1).wait_recv()
+    mine[1] = mine[1] + pair_in[1]
+    both_bits.wait_recv()
+    mine[1] = mine[1] + major_in[0]
+    high_bit = forward(1, 1, away)
+    pair_copy(2).wait_recv()
+    mine[2] = mine[2] + pair_in[2]
+    low_bit = forward(2, 2, near)
+    pair_copy(3).wait_recv()
+    mine[3] = mine[3] + pair_in[3]
+    high_bit.wait_recv()
+    low_bit.wait_recv()
+    out_ref[...] = mine[3] + major_in[1] + major_in[2]
+    for copy in (both_bits, high_bit, low_bit):
         copy.wait_send()
     for step in range(majors):
         pair_copy(step).wait_send()
@@ -313,6 +324,9 @@
         compiler_params=pltpu.CompilerParams(
             collective_id=0, has_side_effects=True, vmem_limit_bytes=48 * 2**20
         ),
+        cost_estimate=pl.CostEstimate(
+            flops=6 * matrix.size * width, bytes_accessed=10 * matrix.size, transcendentals=0
+        ),
     )(matrix, high, low)
 
 
@@ -413,6 +427,7 @@
         compiler_params=pltpu.CompilerParams(
             collective_id=1, has_side_effects=True, vmem_limit_bytes=24 * 2**20
         ),
+        cost_estimate=pl.CostEstimate(flops=0, bytes_accessed=100 * value.size * 4, transcendentals=0),
     )(value.reshape(devices, depth, lanes))
     return total.reshape(value.shape)
 
@@ -463,14 +478,16 @@
     result_mask_two = lax.dynamic_slice_in_dim(mask_two, result_start, local_rows)[:, None]
 
     both = jnp.concatenate([local_one, local_two], axis=1)
-    moves = [(f, (f % row_count) * col_count + f // row_count) for f in range(row_count * col_count)]
-    resident = lax.ppermute(both, ("row", "col"), moves)
-    if local_rows % 128 == 0:
+    late = both
+    if local_rows % 128 == 0 and row_count // 2 == 4:
         high, low = gather_columns(both.T, col_count)
+        high, late = lax.optimization_barrier((high, both))
         product = product_rows(ancestor_inverse, high, low, row_count).T
     else:
         gathered = lax.all_gather(both, "col", axis=0, tiled=True)
         product = scatter_rows(contract_rows(ancestor_inverse, gathered, lax.Precision.HIGH), row_count)
+    moves = [(f, (f % row_count) * col_count + f // row_count) for f in range(row_count * col_count)]
+    resident = lax.ppermute(late, ("row", "col"), moves)
     resident_one = resident[:, :width]
     resident_two = resident[:, width:]
     inverse_one = -product[:, :width] * result_mask_one

time: 209 us -> 202 us (0.967)
  Pallas kernels: 181 us -> 174 us
    pallas_call x1, Pallas kernels: 57.4 us -> 23 us  [gather_columns(): pl.pallas_call(functools.partial(gather_kernel, cols, parts), out_shape=[...]
    pallas_call x1, Pallas kernels: 96.1 us -> 122 us  [product_rows(): pl.pallas_call(functools.partial(product_kernel, rows), out_shape=jax.Sha...]
  transfers between devices with their start and end apart: 2 -> 2, of which waited for: 1 -> 1; matrix products, arithmetic and copies ran while one was open for 2% -> 2% of each run, Pallas kernels for 74% -> 60%
where the time goes in v4:
time: 202 us
  Pallas kernels  174 us (86%)
  matrix products  9.08 us (4%)
  waiting for transfers between devices  7.69 us (4%)
  starting transfers between devices  4.36 us (2%)
  local copies, waits for them, and re-layouts  3.29 us (2%)
  other arithmetic  2.4 us (1%)
    pallas_call x1, Pallas kernels, product_rows(): pl.pallas_call(functools.partial(product_kernel, rows), out_shape=jax.Sha...  122 us
    pallas_call x1, Pallas kernels, sum_everywhere(): pl.pallas_call(functools.partial(sum_kernel, rows, cols), out_shape=jax.S...  29 us
    pallas_call x1, Pallas kernels, gather_columns(): pl.pallas_call(functools.partial(gather_kernel, cols, parts), out_shape=[...  23 us
    all_to_all x1, waiting for transfers between devices, deliver(): lax.all_to_all(outgoing, 'col', split_axis=0, concat_axis=0, tiled=True)  7.68 us
  transfers between devices with their start and end apart: 2, of which 1 were waited for; matrix products, arithmetic and copies ran while one was open for 2% of the time, Pallas kernels for 60%

profile of v4, /device:TPU:0, one launch (start us, length us, event | category | flops | bytes accessed | tf_op | source)
XLA Modules:
  0.0 201.8 jit_solution(742402828323211478)
XLA Ops:
  0.6 0.0 copy-start
  0.7 0.9 add_select_fusion.1
  1.6 0.8 add_select_fusion.3
  2.4 1.4 fusion.15
  3.8 1.3 fusion.12
  5.1 0.1 fusion.36
  5.2 0.1 broadcast_multiply_fusion
  5.3 0.1 broadcast_multiply_fusion.1
  5.5 0.2 pad_maximum_fusion
  5.7 0.3 copy.33
  5.9 23.0 %shard_map.128 = (bf16[512,1536]{1,0:T(8,128)(2,1)S(1)}, bf16[512,1536]{1,0:T(8,128)(2,1)S(1)}) custom-call(f32[2,256,384]{2,1,0:T(8,128)S(1)} %bitcast.51), custom_call_target="tpu_custom_call" | custom-call | tf_op jit(solution)/shard_map/pallas_call | solution.py:192
  29.0 0.7 collective-permute-start
  29.7 122.0 %shard_map.129 = f32[512,384]{1,0:T(8,128)S(1)} custom-call(f32[1536,3072]{1,0:T(8,128)} %matrix_ref.1, bf16[512,1536]{1,0:T(8,128)(2,1)S(1)} %get-tuple-element.10.high_ref, bf16[512,1536]{1,0:T(8,128)(2,1)S(1)} %get-tuple-element.11.low_ref), custom_call_target="tpu_custom_call" | custom-call | flops 14495514624 | bytes 47185920 | tf_op jit(solution)/shard_map/pallas_call | solution.py:307
  151.8 0.6 fusion.7
  152.4 0.2 copy.36
  152.6 0.2 reduce_window_sum.11
  152.8 0.7 fusion.16
  153.5 0.9 copy.38
  154.4 3.7 %all-to-all-start = ((f32[4,2,64,256]{3,2,1,0:T(8,128)}), f32[4,2,64,256]{3,2,1,0:T(8,128)S(1)}, u32[]{:S(2)}, u32[]{:S(2)}) async-start(f32[4,2,64,256]{3,2,1,0:T(8,128)} %copy.38), calls=%async_computation | async-start | bytes 1048576 | tf_op jit(solution)/shard_map/all_to_all | solution.py:449
  158.0 0.9 copy.39
  159.0 7.7 %all-to-all-done = f32[4,2,64,256]{3,2,1,0:T(8,128)S(1)} async-done(((f32[4,2,64,256]{3,2,1,0:T(8,128)}), f32[4,2,64,256]{3,2,1,0:T(8,128)S(1)}, u32[]{:S(2)}, u32[]{:S(2)}) %all-to-all-start) | async-done | bytes 524320 | tf_op jit(solution)/shard_map/all_to_all | solution.py:449
  166.7 0.8 fusion.19
  167.5 0.6 fusion.24
  168.2 0.8 fusion.22
  169.0 29.0 %shard_map.130 = f32[32,48,128]{2,1,0:T(8,128)S(1)} custom-call(f32[32,48,128]{2,1,0:T(8,128)S(1)} %bitcast.52), custom_call_target="tpu_custom_call" | custom-call | bytes 78643200 | tf_op jit(solution)/shard_map/pallas_call | solution.py:413
  198.0 0.1 slice_bitcast_fusion.1
  198.1 0.6 convolution_subtract_fusion
  198.7 0.6 convolution_subtract_fusion.1
  199.3 0.0 copy-start.3
  199.3 0.4 fusion.9
  199.7 1.3 fusion.8
  201.0 0.8 copy.53
  (26 shorter events, 0.2 us)
Async XLA Ops:
  0.6 151.1 %copy-start = (f32[256,256]{1,0:T(8,128)S(1)}, f32[256,256]{1,0:T(8,128)}, u32[]{:S(2)}) copy-start(f32[256,256]{1,0:T(8,128)} %param.15) | copy-start | bytes 786436
  0.6 4.6 %copy-start.5 = (f32[384,256]{1,0:T(8,128)S(1)}, f32[384,256]{1,0:T(8,128)}, u32[]{:S(2)}) copy-start(f32[384,256]{1,0:T(8,128)} %param.13) | copy-start | bytes 1179652
  0.7 4.7 %copy-start.6 = (f32[384,256]{1,0:T(8,128)S(1)}, f32[384,256]{1,0:T(8,128)}, u32[]{:S(2)}) copy-start(f32[384,256]{1,0:T(8,128)} %param.10) | copy-start | bytes 1179652
  5.1 24.6 %copy-start.7 = (s32[6,1]{0,1:T(1,128)S(1)}, s32[6,1]{0,1:T(1,128)}, u32[]{:S(2)}) copy-start(s32[6,1]{0,1:T(1,128)} %param.17) | copy-start | bytes 76
  29.0 137.7 %collective-permute-start = (f32[384,512]{1,0:T(8,128)S(1)}, f32[384,512]{1,0:T(8,128)S(1)}, u32[]{:S(2)}, u32[]{:S(2)}) collective-permute-start(f32[384,512]{1,0:T(8,128)S(1)} %get-tuple-element.12), channel_id=1, source_target_pairs={{0,0},{1,4},{2,8},{3,12},{4,16},{5,20},{6,24},{7,28},{8,1},{9,5},{... | collective-permute-start | bytes 2359304 | tf_op jit(solution)/shard_map/ppermute | solution.py:490
  154.4 12.3 %all-to-all-start = ((f32[4,2,64,256]{3,2,1,0:T(8,128)}), f32[4,2,64,256]{3,2,1,0:T(8,128)S(1)}, u32[]{:S(2)}, u32[]{:S(2)}) async-start(f32[4,2,64,256]{3,2,1,0:T(8,128)} %copy.38), calls=%async_computation | async-start | bytes 1048576 | tf_op jit(solution)/shard_map/all_to_all | solution.py:449
  167.5 30.6 %copy-start.1 = (f32[256,256]{1,0:T(8,128)S(1)}, f32[256,256]{1,0:T(8,128)}, u32[]{:S(2)}) copy-start(f32[256,256]{1,0:T(8,128)} %param.16) | copy-start | bytes 786436
  167.5 31.2 %copy-start.2 = (f32[256,256]{1,0:T(8,128)S(1)}, f32[256,256]{1,0:T(8,128)}, u32[]{:S(2)}) copy-start(f32[256,256]{1,0:T(8,128)} %param.12) | copy-start | bytes 786436
  199.3 2.5 %copy-start.3 = (f32[256,256]{1,0:T(8,128)}, f32[256,256]{1,0:T(8,128)S(1)}, u32[]{:S(2)}) copy-start(f32[256,256]{1,0:T(8,128)S(1)} %convolution_subtract_fusion.1) | copy-start | bytes 786436
  199.7 2.1 %copy-start.4 = (f32[256,256]{1,0:T(8,128)}, f32[256,256]{1,0:T(8,128)S(1)}, u32[]{:S(2)}) copy-start(f32[256,256]{1,0:T(8,128)S(1)} %fusion.9) | copy-start | bytes 786436
